TPU v7x, 32 devices: a whole 2x2x4 slice. The times are simulated.
32 devices in a mesh: ctx: 8 (over y, x, core), head: 4 (over z).
Axes of the slice: x: 2, y: 2, z: 4, core: 2. Of those that a mesh axis runs over, the one named last changes fastest.
Arguments:
- row_query: bfloat16 [8192, 3072], P('ctx', 'head'), may hold values from -160 to 160
- row_key: bfloat16 [8192, 3072], P('ctx', 'head'), may hold values from -5 to 5
- row_value: bfloat16 [8192, 3072], P('ctx', 'head'), may hold values from -6 to 6
- row_cotangent: bfloat16 [8192, 3072], P('ctx', 'head'), may hold values from -6 to 6
- row_mask: int32 [64, 9], replicated, may hold values from 0 to 1, as said below
- col_query: bfloat16 [8192, 3072], P('ctx', 'head'), may hold values from -160 to 160
- col_key: bfloat16 [8192, 3072], P('ctx', 'head'), may hold values from -5 to 5
- col_value: bfloat16 [8192, 3072], P('ctx', 'head'), may hold values from -6 to 6
- col_cotangent: bfloat16 [8192, 3072], P('ctx', 'head'), may hold values from -6 to 6
- col_mask: int32 [64, 64], replicated, may hold values from 0 to 1, as said below
Outputs:
- row_output: bfloat16 [8192, 3072], P('ctx', 'head')
- row_dquery: bfloat16 [8192, 3072], P('ctx', 'head')
- row_dkeys: bfloat16 [8192, 3072], P('ctx', 'head')
- row_dvalues: bfloat16 [8192, 3072], P('ctx', 'head')
- col_output: bfloat16 [8192, 3072], P('ctx', 'head')
- col_dquery: bfloat16 [8192, 3072], P('ctx', 'head')
- col_dkeys: bfloat16 [8192, 3072], P('ctx', 'head')
- col_dvalues: bfloat16 [8192, 3072], P('ctx', 'head')
Inputs may be any that keep to these rules, and one draw needn't show every extreme that they name: row_mask[r, 4] = 1 for every r, row_mask[r, 3] = 1 for even r and row_mask[r, 5] = 1 for odd r; entries that point outside the grid are ignored. col_mask[r, r] = 1 for every r and col_mask[r, r - 1] = 1 for r >= 1.
All inputs are finite; a program needn't handle non-finite values.
Results may differ from a plain program's by a relative error of at most 0.022.
Values may be sent and summed in bfloat16 or wider, within the bound.
No kernel may reach another device: no remote copies, remote signals or barrier semaphores. Data moves between devices by JAX's collectives and lax.ppermute only.
A program may use at most 192 MiB of HBM per device.

v0:
```python
import jax
import jax.numpy as jnp
from jax import lax
from jax.sharding import PartitionSpec as P

HEAD_DIM = 128
GRIDC = 128
masked_score = -1e30


def padded_2(array, sides, width):
    for axis, dim in sides:
        size, length = (lax.axis_size(axis), array.shape[dim])
        up = [(i, (i + 1) % size) for i in range(size - 1)]
        down = [(j, i) for i, j in up]
        last = lax.slice_in_dim(array, length - width, length, axis=dim)
        initial = lax.slice_in_dim(array, 0, width, axis=dim)
        before = lax.ppermute(last, axis, up)
        after = lax.ppermute(initial, axis, down)
        array = jnp.concatenate([before, array, after], axis=dim)
    return array


def passed_along(block, axis, distance):
    devices = range(lax.axis_size(axis))
    route = [(i - distance, i) for i in devices if i - distance in devices]
    return lax.ppermute(block, axis, route)


def attend_block(queries, key_block, value_block, cotangent, allowed):
    scale = queries.shape[-1] ** (-0.5)
    scores = (
        jnp.einsum("bnd,bmd->bnm", queries, key_block, preferred_element_type=jnp.float32) * scale
    )
    scores = jnp.where(allowed, scores, masked_score)
    row_max = jnp.max(scores, axis=-1, keepdims=True)
    exp_terms = jnp.where(allowed, jnp.exp(scores - row_max), 0.0)
    attn_prob = exp_terms / jnp.sum(exp_terms, axis=-1, keepdims=True)
    prob_low = attn_prob.astype(jnp.bfloat16)
    output = jnp.einsum(
        "bnm,bmd->bnd", prob_low, value_block, preferred_element_type=jnp.float32
    ).astype(jnp.bfloat16)
    d_prob = jnp.einsum("bnd,bmd->bnm", cotangent, value_block, preferred_element_type=jnp.float32)
    delta_sum = jnp.sum(
        cotangent.astype(jnp.float32) * output.astype(jnp.float32), axis=-1, keepdims=True
    )
    d_scores = (attn_prob * (d_prob - delta_sum)).astype(jnp.bfloat16)
    grad_query = (
        jnp.einsum("bnm,bmd->bnd", d_scores, key_block, preferred_element_type=jnp.float32) * scale
    ).astype(jnp.bfloat16)
    grad_keys = (
        jnp.einsum("bnm,bnd->bmd", d_scores, queries, preferred_element_type=jnp.float32) * scale
    )
    grad_values = jnp.einsum(
        "bnm,bnd->bmd", prob_low, cotangent, preferred_element_type=jnp.float32
    )
    return (output, grad_query, grad_keys, grad_values)


def row_allowed(mask_rows, first, nrows, window, band, total_rows, grid_cols):
    query_rows = first + jnp.arange(nrows)[:, None]
    block_rows = query_rows + jnp.arange(window)[None, :] - band
    valid = (block_rows >= 0) & (block_rows < total_rows) & (mask_rows == 1)
    outside = (query_rows < 0) | (query_rows >= total_rows)
    valid = valid | outside
    return jnp.repeat(valid, grid_cols, axis=1)[:, None, :]


def row_pass(queries, pairs, cotangent, allowed, nrows, band, window, grid_cols):
    head_dim = HEAD_DIM
    heads = queries.shape[1] // head_dim
    head_queries = queries.reshape(nrows, grid_cols, heads, head_dim).transpose(2, 0, 1, 3)
    head_cotangent = cotangent.reshape(nrows, grid_cols, heads, head_dim).transpose(2, 0, 1, 3)
    head_pairs = pairs.reshape(2, nrows + 2 * band, grid_cols, heads, head_dim).transpose(
        3, 0, 1, 2, 4
    )

    def one_head(operands):
        head_q, head_kv, head_cot = operands
        windows = jnp.stack([head_kv[:, offset : offset + nrows] for offset in range(window)], 2)
        windows = windows.reshape(2, nrows, window * grid_cols, head_dim)
        output, grad_query, grad_keys, grad_values = attend_block(
            head_q, windows[0], windows[1], head_cot, allowed
        )
        grads = jnp.stack([grad_keys, grad_values]).reshape(2, nrows, window, grid_cols, head_dim)
        accum = jnp.zeros((2, nrows + 2 * band, grid_cols, head_dim), jnp.float32)
        for offset in range(window):
            accum = accum.at[:, offset : offset + nrows].add(grads[:, :, offset])
        return (output, grad_query, accum)

    return lax.map(one_head, (head_queries, head_pairs, head_cotangent))


def body(
    row_query,
    row_key,
    row_value,
    row_cotangent,
    row_mask,
    col_query,
    col_key,
    col_value,
    col_cotangent,
    col_mask,
):
    head_dim = HEAD_DIM
    grid_cols = GRIDC
    tokens = row_query.shape[0]
    rows_here = tokens // grid_cols
    window = row_mask.shape[1]
    band = (window - 1) // 2
    row_feat = row_query.shape[1]
    first_row = lax.axis_index("ctx") * rows_here
    total_rows = rows_here * lax.axis_size("ctx")
    key_value = jnp.stack([row_key, row_value])
    padded = padded_2(key_value, (("ctx", 1),), band * grid_cols)
    mask_rows = lax.dynamic_slice_in_dim(row_mask, first_row, rows_here, 0)
    allowed_rows = row_allowed(mask_rows, first_row, rows_here, window, band, total_rows, grid_cols)
    outputs, grad_queries, accums = row_pass(
        row_query, padded, row_cotangent, allowed_rows, rows_here, band, window, grid_cols
    )
    lower_rim = accums[:, :, :band]
    upper_rim = accums[:, :, band + rows_here :]
    own_grads = accums[:, :, band : band + rows_here]
    from_next = passed_along(lower_rim.astype(jnp.bfloat16), "ctx", -1).astype(lower_rim.dtype)
    from_prev = passed_along(upper_rim.astype(jnp.bfloat16), "ctx", 1).astype(upper_rim.dtype)
    own_grads = own_grads.at[:, :, rows_here - band :].add(from_next)
    own_grads = own_grads.at[:, :, :band].add(from_prev)
    own_grads = own_grads.transpose(1, 2, 3, 0, 4).reshape(2, tokens, row_feat).astype(jnp.bfloat16)
    row_output = outputs.transpose(1, 2, 0, 3).reshape(tokens, row_feat)
    row_dquery = grad_queries.transpose(1, 2, 0, 3).reshape(tokens, row_feat)
    row_dkeys = own_grads[0]
    row_dvalues = own_grads[1]
    col_feat = col_query.shape[1]
    n_ctx = lax.axis_size("ctx")
    grid_rows = rows_here * n_ctx
    stacked = jnp.stack([col_query, col_key, col_value, col_cotangent]).reshape(
        4, rows_here, grid_cols, col_feat
    )
    moved = lax.all_to_all(stacked, "ctx", split_axis=2, concat_axis=1, tiled=True)
    cols_here = moved.shape[2]
    all_heads = moved.shape[3] // head_dim
    batched = moved.reshape(4, grid_rows, cols_here, all_heads, head_dim).transpose(0, 2, 3, 1, 4)
    batched = batched.reshape(4, cols_here * all_heads, grid_rows, head_dim)
    allowed_cols = (col_mask == 1)[None]
    output, grad_query, grad_keys, grad_values = attend_block(
        batched[0], batched[1], batched[2], batched[3], allowed_cols
    )
    results = jnp.stack(
        [output, grad_query, grad_keys.astype(jnp.bfloat16), grad_values.astype(jnp.bfloat16)]
    )
    results = results.reshape(4, cols_here, all_heads, grid_rows, head_dim).transpose(0, 3, 1, 2, 4)
    results = results.reshape(4, grid_rows, cols_here, all_heads * head_dim)
    returned = lax.all_to_all(results, "ctx", split_axis=1, concat_axis=2, tiled=True)
    returned = returned.reshape(4, tokens, col_feat)
    return (
        row_output,
        row_dquery,
        row_dkeys,
        row_dvalues,
        returned[0],
        returned[1],
        returned[2],
        returned[3],
    )


def solution(mesh):
    return jax.shard_map(
        body,
        mesh=mesh,
        in_specs=(
            P("ctx", "head"),
            P("ctx", "head"),
            P("ctx", "head"),
            P("ctx", "head"),
            P(),
            P("ctx", "head"),
            P("ctx", "head"),
            P("ctx", "head"),
            P("ctx", "head"),
            P(),
        ),
        out_specs=(
            P("ctx", "head"),
            P("ctx", "head"),
            P("ctx", "head"),
            P("ctx", "head"),
            P("ctx", "head"),
            P("ctx", "head"),
            P("ctx", "head"),
            P("ctx", "head"),
        ),
        check_vma=False,
    )
```

profile of v0, /device:TPU:11, one launch (start us, length us, event | category | flops | bytes accessed | tf_op | source)
XLA Modules:
  0.0 450.1 jit_solution(2632079442033608553)
XLA Ops:
  0.6 3.7 pad_maximum_fusion.2
  4.4 6.3 %copy.209 = bf16[4,8,128,768]{3,1,0,2:T(8,128)(2,1)} copy(bf16[4,8,128,768]{3,2,1,0:T(8,128)(2,1)S(1)} %pad_maximum_fusion.2) | data formatting | bytes 12582912 | tf_op jit(solution)/shard_map/stack | solution.py:137
  10.6 5.8 %all-to-all-start = ((bf16[4,8,128,768]{3,1,0,2:T(8,128)(2,1)}), bf16[4,8,128,768]{3,1,0,2:T(8,128)(2,1)}, u32[]{:S(2)}, u32[]{:S(2)}) async-start(bf16[4,8,128,768]{3,1,0,2:T(8,128)(2,1)} %copy.209), calls=%async_computation | async-start | bytes 12582912 | tf_op jit(solution)/shard_map/all_to_all | solution.py:140
  20.5 4.4 collective-permute-start
  24.9 2.6 copy.197
  27.5 3.0 copy.263
  30.5 2.6 copy.199
  33.1 3.0 copy.265
  36.3 83.7 %collective-permute-done.1 = bf16[2,512,768]{2,1,0:T(8,128)(2,1)} collective-permute-done((bf16[2,512,768]{2,1,0:T(8,128)(2,1)}, bf16[2,512,768]{2,1,0:T(8,128)(2,1)}, u32[]{:S(2)}, u32[]{:S(2)}) %collective-permute-start.1) | collective-permute-done | bytes 1572896 | tf_op jit(solution)/shard_map/ppermute | solution.py:19
  120.0 5.1 %pad_maximum_fusion.1 = bf16[2,2048,768]{2,1,0:T(8,128)(2,1)} fusion(bf16[2,512,768]{2,1,0:T(8,128)(2,1)} %collective-permute-done.1, bf16[1,1024,768]{2,1,0:T(8,128)(2,1)S(1)} %bitcast.375, bf16[1,1024,768]{2,1,0:T(8,128)(2,1)S(1)} %bitcast.373, bf16[2,512,768]{2,1,0:T(8,128)(2,1)} %collective-permute-done), kind=kLoop, calls=%fused_computation.102 | loop fusion | flops 25165824 | bytes 12582912 | tf_op jit(solution)/shard_map/concatenate | solution.py:20
  125.2 8.7 %copy.198 = bf16[2,2048,768]{1,2,0:T(8,128)(2,1)} copy(bf16[2,2048,768]{2,1,0:T(8,128)(2,1)} %pad_maximum_fusion.1) | data formatting | bytes 12582912 | tf_op jit(solution)/shard_map/concatenate | solution.py:20
  133.8 7.7 %copy.264 = bf16[192,8,16,128]{3,2,1,0:T(8,128)(2,1)} copy(bf16[192,8,16,128]{3,1,2,0:T(8,128)(2,1)} %bitcast.366) | data formatting | bytes 12582912
  141.6 10.6 %copy.211 = bf16[4,8,8,16,768]{4,3,2,1,0:T(8,128)(2,1)} copy(bf16[4,8,8,16,768]{4,2,0,3,1:T(8,128)(2,1)} %bitcast.14) | data formatting | bytes 12582912 | tf_op jit(solution)/shard_map/all_to_all | solution.py:140
  152.2 13.6 %reshape.576 = bf16[4,64,16,6,128]{4,3,2,1,0:T(8,128)(2,1)} reshape(bf16[4,8,8,16,768]{4,3,2,1,0:T(8,128)(2,1)} %copy.211) | data formatting | bytes 12582912 | tf_op jit(solution)/shard_map/reshape | solution.py:143
  165.8 5.8 %fusion.85 = (bf16[1,16,6,64,128]{4,2,1,3,0:T(8,128)(2,1)S(1)}, bf16[1,16,6,64,128]{4,2,1,3,0:T(8,128)(2,1)S(1)}, bf16[1,16,6,64,128]{4,2,1,3,0:T(8,128)(2,1)S(1)}, bf16[1,16,6,64,128]{4,2,1,3,0:T(8,128)(2,1)S(1)}) fusion(bf16[4,16,6,64,128]{4,2,1,3,0:T(8,128)(2,1)} %bitcast.364), kind=kLoop, calls=%fused_computation.144 | loop fusion | bytes 12582912 | tf_op jit(solution)/shard_map/slice | solution.py:147
  177.9 3.2 fusion.89
  181.2 3.1 convolution_convert_fusion.1
  193.7 4.4 maximum_bitcast_fusion
  198.1 13.8 %reshape.577 = bf16[4,64,16,768]{3,2,1,0:T(8,128)(2,1)} reshape(bf16[4,64,16,6,128]{4,3,2,1,0:T(8,128)(2,1)} %maximum_bitcast_fusion) | data formatting | bytes 12582912 | tf_op jit(solution)/shard_map/reshape | solution.py:153
  211.9 6.3 %copy.223 = bf16[4,64,16,768]{3,2,0,1:T(8,128)(2,1)} copy(bf16[4,64,16,768]{3,2,1,0:T(8,128)(2,1)} %reshape.577) | data formatting | bytes 12582912 | tf_op jit(solution)/shard_map/reshape | solution.py:153
  218.2 4.7 %all-to-all-start.1 = ((bf16[4,64,16,768]{3,2,0,1:T(8,128)(2,1)}), bf16[4,64,16,768]{3,2,0,1:T(8,128)(2,1)}, u32[]{:S(2)}, u32[]{:S(2)}) async-start(bf16[4,64,16,768]{3,2,0,1:T(8,128)(2,1)} %copy.223), calls=%async_computation.1 | async-start | bytes 12582912 | tf_op jit(solution)/shard_map/all_to_all | solution.py:154
  222.9 160.0 %while.29 = (s32[]{:T(128)}, bf16[6,8,128,128]{2,3,1,0:T(8,128)(2,1)}, bf16[6,8,128,128]{3,2,1,0:T(8,128)(2,1)}, f32[6,2,16,128,128]{4,3,2,1,0:T(8,128)}, bf16[6...) while((s32[]{:T(128)}, ...), condition=%wide.region_4.5_spmd.clone, body=%wide.region_0.4_spmd.clone.sunk | while | flops 1831469184 | bytes 216832256 | solution.py:91
  226.0 2.4 fusion.165
  229.8 5.7 %fusion.166 = (f32[8,128]{1,0:T(8,128)S(1)}, f32[8,128,1152]{2,1,0:T(8,128)}) fusion(bf16[8,1152,128]{2,1,0:T(8,128)(2,1)} %bitcast.362, pred[8,1152]{1,0:T(8,128)(4,1)S(1)} %broadcast_bitcast_fusion.2, bf16[1,8,128,128]{3,2,1,0:T(8,128)(2,1)S(1)} %copy.288), kind=kOutput, calls=%fused_computation.143.clone.1 | convolution fusion | flops 307889280 | bytes 7353344 | tf_op jit(solution)/shard_map/while/body/eval_jaxpr/sub | solution.py:37
  235.5 2.8 fusion.167
  252.7 2.4 fusion.165
  256.4 5.7 %fusion.166 = (f32[8,128]{1,0:T(8,128)S(1)}, f32[8,128,1152]{2,1,0:T(8,128)}) fusion(bf16[8,1152,128]{2,1,0:T(8,128)(2,1)} %bitcast.362, pred[8,1152]{1,0:T(8,128)(4,1)S(1)} %broadcast_bitcast_fusion.2, bf16[1,8,128,128]{3,2,1,0:T(8,128)(2,1)S(1)} %copy.288), kind=kOutput, calls=%fused_computation.143.clone.1 | convolution fusion | flops 307889280 | bytes 7353344 | tf_op jit(solution)/shard_map/while/body/eval_jaxpr/sub | solution.py:37
  262.1 2.8 fusion.167
  279.3 2.4 fusion.165
  283.0 5.7 %fusion.166 = (f32[8,128]{1,0:T(8,128)S(1)}, f32[8,128,1152]{2,1,0:T(8,128)}) fusion(bf16[8,1152,128]{2,1,0:T(8,128)(2,1)} %bitcast.362, pred[8,1152]{1,0:T(8,128)(4,1)S(1)} %broadcast_bitcast_fusion.2, bf16[1,8,128,128]{3,2,1,0:T(8,128)(2,1)S(1)} %copy.288), kind=kOutput, calls=%fused_computation.143.clone.1 | convolution fusion | flops 307889280 | bytes 7353344 | tf_op jit(solution)/shard_map/while/body/eval_jaxpr/sub | solution.py:37
  288.7 2.8 fusion.167
  305.9 2.4 fusion.165
  309.7 5.7 %fusion.166 = (f32[8,128]{1,0:T(8,128)S(1)}, f32[8,128,1152]{2,1,0:T(8,128)}) fusion(bf16[8,1152,128]{2,1,0:T(8,128)(2,1)} %bitcast.362, pred[8,1152]{1,0:T(8,128)(4,1)S(1)} %broadcast_bitcast_fusion.2, bf16[1,8,128,128]{3,2,1,0:T(8,128)(2,1)S(1)} %copy.288), kind=kOutput, calls=%fused_computation.143.clone.1 | convolution fusion | flops 307889280 | bytes 7353344 | tf_op jit(solution)/shard_map/while/body/eval_jaxpr/sub | solution.py:37
  315.4 2.8 fusion.167
  336.3 5.7 %fusion.166 = (f32[8,128]{1,0:T(8,128)S(1)}, f32[8,128,1152]{2,1,0:T(8,128)}) fusion(bf16[8,1152,128]{2,1,0:T(8,128)(2,1)} %bitcast.362, pred[8,1152]{1,0:T(8,128)(4,1)S(1)} %broadcast_bitcast_fusion.2, bf16[1,8,128,128]{3,2,1,0:T(8,128)(2,1)S(1)} %copy.288), kind=kOutput, calls=%fused_computation.143.clone.1 | convolution fusion | flops 307889280 | bytes 7353344 | tf_op jit(solution)/shard_map/while/body/eval_jaxpr/sub | solution.py:37
  342.0 2.8 fusion.167
  359.2 2.4 fusion.165
  363.0 5.7 %fusion.166 = (f32[8,128]{1,0:T(8,128)S(1)}, f32[8,128,1152]{2,1,0:T(8,128)}) fusion(bf16[8,1152,128]{2,1,0:T(8,128)(2,1)} %bitcast.362, pred[8,1152]{1,0:T(8,128)(4,1)S(1)} %broadcast_bitcast_fusion.2, bf16[1,8,128,128]{3,2,1,0:T(8,128)(2,1)S(1)} %copy.288), kind=kOutput, calls=%fused_computation.143.clone.1 | convolution fusion | flops 307889280 | bytes 7353344 | tf_op jit(solution)/shard_map/while/body/eval_jaxpr/sub | solution.py:37
  368.7 2.8 fusion.167
  383.0 6.2 %convert.4 = bf16[6,2,16,128,128]{4,3,2,1,0:T(8,128)(2,1)S(1)} convert(f32[6,2,16,128,128]{4,3,2,1,0:T(8,128)} %get-tuple-element.300) | non-fusion elementwise | flops 3145728 | bytes 18874368 | tf_op jit(solution)/shard_map/convert.1
  393.0 4.7 %collective-permute-start.3 = (bf16[6,2,4,128,128]{4,3,2,1,0:T(8,128)(2,1)}, bf16[6,2,4,128,128]{4,3,2,1,0:T(8,128)(2,1)}, u32[]{:S(2)}, u32[]{:S(2)}) collective-permute-start(bf16[6,2,4,128,128]{4,3,2,1,0:T(8,128)(2,1)} %get-tuple-element.424), channel_id=1, source_target_pairs={{0,4},{4,8},{8,12},{12,16},{16,20},{20,24},{24,28},{1,5},{5,9},{9,... | collective-permute-start | bytes 4718600 | tf_op jit(solution)/shard_map/ppermute | solution.py:27
  397.7 6.3 %slice.552 = f32[6,2,8,128,128]{4,3,2,1,0:T(8,128)} slice(f32[6,2,16,128,128]{4,3,2,1,0:T(8,128)} %get-tuple-element.300), slice={[0:6], [0:2], [4:12], [0:128], [0:128]} | slice | bytes 12582912 | tf_op jit(solution)/shard_map/slice | solution.py:124
  405.1 3.9 copy.241
  409.0 4.4 copy_bitcast_fusion.5
  413.3 16.9 %collective-permute-done.2 = bf16[6,2,4,128,128]{4,3,2,1,0:T(8,128)(2,1)} collective-permute-done((bf16[6,2,4,128,128]{4,3,2,1,0:T(8,128)(2,1)}, bf16[6,2,4,128,128]{4,3,2,1,0:T(8,128)(2,1)}, u32[]{:S(2)}, u32[]{:S(2)}) %collective-permute-start.2) | collective-permute-done | bytes 1572896 | tf_op jit(solution)/shard_map/ppermute | solution.py:27
  430.2 2.8 add_dynamic-update-slice_fusion
  438.4 2.6 copy_bitcast_fusion.3
  441.0 3.4 copy.224
  (274 shorter events, 131.4 us)
Async XLA Ops:
  10.6 5.8 %copy-start.3 = (bf16[1024,768]{1,0:T(8,128)(2,1)S(1)}, bf16[1024,768]{1,0:T(8,128)(2,1)}, u32[]{:S(2)}) copy-start(bf16[1024,768]{1,0:T(8,128)(2,1)} %param.35) | copy-start | bytes 4718596
  10.6 5.8 %copy-start.4 = (bf16[1024,768]{1,0:T(8,128)(2,1)S(1)}, bf16[1024,768]{1,0:T(8,128)(2,1)}, u32[]{:S(2)}) copy-start(bf16[1024,768]{1,0:T(8,128)(2,1)} %param.36) | copy-start | bytes 4718596
  10.6 130.9 %all-to-all-start = ((bf16[4,8,128,768]{3,1,0,2:T(8,128)(2,1)}), bf16[4,8,128,768]{3,1,0,2:T(8,128)(2,1)}, u32[]{:S(2)}, u32[]{:S(2)}) async-start(bf16[4,8,128,768]{3,1,0,2:T(8,128)(2,1)} %copy.209), calls=%async_computation | async-start | bytes 12582912 | tf_op jit(solution)/shard_map/all_to_all | solution.py:140
  18.2 101.8 %collective-permute-start.1 = (bf16[2,512,768]{2,1,0:T(8,128)(2,1)}, bf16[2,512,768]{2,1,0:T(8,128)(2,1)}, u32[]{:S(2)}, u32[]{:S(2)}) collective-permute-start(bf16[2,512,768]{2,1,0:T(8,128)(2,1)} %get-tuple-element.429), channel_id=1, source_target_pairs={{4,0},{8,4},{12,8},{16,12},{20,16},{24,20},{28,24},{5,1},{9,5},{13... | collective-permute-start | bytes 4718600 | tf_op jit(solution)/shard_map/ppermute | solution.py:19
  20.5 99.5 %collective-permute-start = (bf16[2,512,768]{2,1,0:T(8,128)(2,1)}, bf16[2,512,768]{2,1,0:T(8,128)(2,1)}, u32[]{:S(2)}, u32[]{:S(2)}) collective-permute-start(bf16[2,512,768]{2,1,0:T(8,128)(2,1)} %get-tuple-element.428), channel_id=1, source_target_pairs={{0,4},{4,8},{8,12},{12,16},{16,20},{20,24},{24,28},{1,5},{5,9},{9,... | collective-permute-start | bytes 4718600 | tf_op jit(solution)/shard_map/ppermute | solution.py:18
  33.1 3.0 copy-start.8
  33.1 3.2 copy-start.9
  181.2 3.1 copy-start.6
  181.2 3.3 copy-start.7
  181.2 4.3 copy-start.10
  218.2 222.7 %all-to-all-start.1 = ((bf16[4,64,16,768]{3,2,0,1:T(8,128)(2,1)}), bf16[4,64,16,768]{3,2,0,1:T(8,128)(2,1)}, u32[]{:S(2)}, u32[]{:S(2)}) async-start(bf16[4,64,16,768]{3,2,0,1:T(8,128)(2,1)} %copy.223), calls=%async_computation.1 | async-start | bytes 12582912 | tf_op jit(solution)/shard_map/all_to_all | solution.py:154
  238.3 2.4 copy-start
  240.8 1.7 copy-start.1
  265.0 2.4 copy-start
  267.4 1.7 copy-start.1
  291.6 2.4 copy-start
  294.0 1.7 copy-start.1
  318.2 2.4 copy-start
  320.7 1.7 copy-start.1
  344.9 2.4 copy-start
  347.3 1.7 copy-start.1
  371.5 2.4 copy-start
  374.0 1.7 copy-start.1
  391.0 39.2 %collective-permute-start.2 = (bf16[6,2,4,128,128]{4,3,2,1,0:T(8,128)(2,1)}, bf16[6,2,4,128,128]{4,3,2,1,0:T(8,128)(2,1)}, u32[]{:S(2)}, u32[]{:S(2)}) collective-permute-start(bf16[6,2,4,128,128]{4,3,2,1,0:T(8,128)(2,1)} %get-tuple-element.425), channel_id=1, source_target_pairs={{4,0},{8,4},{12,8},{16,12},{20,16},{24,20},{28,24},{5,1},{9,5},{13... | collective-permute-start | bytes 4718600 | tf_op jit(solution)/shard_map/ppermute | solution.py:27
  393.0 11.0 %copy-start.5 = (bf16[6,8,128,128]{3,2,1,0:T(8,128)(2,1)S(1)}, bf16[6,8,128,128]{3,2,1,0:T(8,128)(2,1)}, u32[]{:S(2)}) copy-start(bf16[6,8,128,128]{3,2,1,0:T(8,128)(2,1)} %get-tuple-element.299) | copy-start | bytes 4718596
  393.0 40.0 %collective-permute-start.3 = (bf16[6,2,4,128,128]{4,3,2,1,0:T(8,128)(2,1)}, bf16[6,2,4,128,128]{4,3,2,1,0:T(8,128)(2,1)}, u32[]{:S(2)}, u32[]{:S(2)}) collective-permute-start(bf16[6,2,4,128,128]{4,3,2,1,0:T(8,128)(2,1)} %get-tuple-element.424), channel_id=1, source_target_pairs={{0,4},{4,8},{8,12},{12,16},{16,20},{20,24},{24,28},{1,5},{5,9},{9,... | collective-permute-start | bytes 4718600 | tf_op jit(solution)/shard_map/ppermute | solution.py:27
  409.0 21.2 %copy-start.2 = (f32[6,2,8,128,128]{4,3,2,1,0:T(8,128)S(1)}, f32[6,2,8,128,128]{4,3,2,1,0:T(8,128)}, u32[]{:S(2)}) copy-start(f32[6,2,8,128,128]{4,3,2,1,0:T(8,128)} %slice.552) | copy-start | bytes 18874372
where the time goes:
time: 457 us; the launch traced here: 450 us
  local copies, waits for them, and re-layouts  185 us (40%)
  waiting for transfers between devices  101 us (22%)
  matrix products  82.3 us (18%)
  other arithmetic  56.6 us (12%)
  starting transfers between devices  23.7 us (5%)
    ppermute x1, waiting for transfers between devices, padded_2(): after = lax.ppermute(initial, axis, down)  83.7 us
    sub x7, matrix products, attend_block(): exp_terms = jnp.where(allowed, jnp.exp(scores - row_max), 0.0)  37.6 us
    unnamed x29, local copies, waits for them, and re-layouts  34.3 us
    dynamic_slice x24, local copies, waits for them, and re-layouts, row_pass(): return lax.map(one_head, (head_queries, head_pairs, head_cotangent))  22.1 us
    reshape x2, local copies, waits for them, and re-layouts, body(): results = results.reshape(4, grid_rows, cols_here, all_heads * head_dim)  20.1 us
    convert_element_type x6, other arithmetic, attend_block(): prob_low = attn_prob.astype(jnp.bfloat16)  17.1 us
    ppermute x2, waiting for transfers between devices, passed_along(): return lax.ppermute(block, axis, route)  16.9 us
    slice x6, local copies, waits for them, and re-layouts, one_head(): windows[1]  14.1 us
  transfers between devices with their start and end apart: 6, of which 2 were waited for; matrix products, arithmetic and copies ran while one was open for 49% of the time, Pallas kernels for 0%

commit v1 on v0

--- a/solution.py
+++ b/solution.py
@@ -6,6 +6,17 @@
 HEAD_DIM = 128
 GRIDC = 128
 masked_score = -1e30
+
+
+def split_up(shard, dim, devices):
+    before, after = (shard.shape[:dim], shard.shape[dim + 1 :])
+    return jnp.moveaxis(shard.reshape(*before, devices, -1, *after), dim, 0)
+
+
+def joined_along(pieces, dim):
+    shape = list(pieces.shape[1:])
+    shape[dim] *= pieces.shape[0]
+    return jnp.moveaxis(pieces, 0, dim).reshape(shape)
 
 
 def padded_2(array, sides, width):
@@ -137,7 +148,14 @@
     stacked = jnp.stack([col_query, col_key, col_value, col_cotangent]).reshape(
         4, rows_here, grid_cols, col_feat
     )
-    moved = lax.all_to_all(stacked, "ctx", split_axis=2, concat_axis=1, tiled=True)
+    count, here = (lax.axis_size("ctx"), lax.axis_index("ctx"))
+    parts = split_up(stacked, 2, count)
+    outs = [parts[here]]
+    for hop in range(1, count):
+        sent = parts[here ^ hop]
+        outs.append(lax.ppermute(sent, "ctx", [(i_2, i_2 ^ hop) for i_2 in range(count)]))
+    parts = jnp.stack(outs)[here ^ jnp.arange(count)]
+    moved = joined_along(parts, 1)
     cols_here = moved.shape[2]
     all_heads = moved.shape[3] // head_dim
     batched = moved.reshape(4, grid_rows, cols_here, all_heads, head_dim).transpose(0, 2, 3, 1, 4)

time: 457 us -> 454 us (level)
  waiting for transfers between devices: 101 us -> 92.6 us
    ppermute x1, waiting for transfers between devices: 83.7 us -> 0.01 us  [padded_2(): after = lax.ppermute(initial, axis, down)]
    ppermute x0 -> x7, waiting for transfers between devices: none -> 76.7 us  [body(): lax.ppermute(sent, 'ctx', [(i_2, i_2 ^ hop) for i_2 in range(count)])]
    reshape x1 -> x0, local copies, waits for them, and re-layouts: 13.6 us -> none  [body(): moved.reshape(4, grid_rows, cols_here, all_heads, head_dim)]
    all_to_all x1 -> x0, local copies, waits for them, and re-layouts: 10.6 us -> none  [body(): lax.all_to_all(stacked, 'ctx', split_axis=2, concat_axis=1, tiled=True)]
    another operation x1 -> x2, local copies, waits for them, and re-layouts: 6.25 us -> 14.6 us  [the longest x1 13.7 us: body(): moved.reshape(4, grid_rows, cols_here, all_heads, head_dim)]
    unnamed x29 -> x52, local copies, waits for them, and re-layouts: 34.3 us -> 41.1 us
    gather x0 -> x1, local copies, waits for them, and re-layouts: none -> 6.37 us  [body(): parts = jnp.stack(outs)[here ^ jnp.arange(count)]]
    transpose x0 -> x1, local copies, waits for them, and re-layouts: none -> 6.14 us  [joined_along(): return jnp.moveaxis(pieces, 0, dim).reshape(shape)]
  transfers between devices with their start and end apart: 6 -> 12, of which waited for: 2 -> 4; matrix products, arithmetic and copies ran while one was open for 49% -> 69% of each run, Pallas kernels for 0% -> 0%
where the time goes in v1:
time: 454 us; the launch traced here: 446 us
  local copies, waits for them, and re-layouts  186 us (41%)
  waiting for transfers between devices  92.6 us (20%)
  matrix products  81.9 us (18%)
  other arithmetic  58.8 us (13%)
  starting transfers between devices  23.5 us (5%)
    ppermute x7, waiting for transfers between devices, body(): lax.ppermute(sent, 'ctx', [(i_2, i_2 ^ hop) for i_2 in range(count)])  76.7 us
    unnamed x52, local copies, waits for them, and re-layouts  41.1 us
    sub x7, matrix products, attend_block(): exp_terms = jnp.where(allowed, jnp.exp(scores - row_max), 0.0)  36.9 us
    dynamic_slice x24, local copies, waits for them, and re-layouts, row_pass(): return lax.map(one_head, (head_queries, head_pairs, head_cotangent))  22.1 us
    reshape x2, local copies, waits for them, and re-layouts, body(): results = results.reshape(4, grid_rows, cols_here, all_heads * head_dim)  20.2 us
    convert_element_type x6, other arithmetic, attend_block(): prob_low = attn_prob.astype(jnp.bfloat16)  18 us
    ppermute x2, waiting for transfers between devices, passed_along(): return lax.ppermute(block, axis, route)  15.9 us
    slice x6, local copies, waits for them, and re-layouts, one_head(): windows[1]  14.4 us
  transfers between devices with their start and end apart: 12, of which 4 were waited for; matrix products, arithmetic and copies ran while one was open for 69% of the time, Pallas kernels for 0%

profile of v1, /device:TPU:11, one launch (start us, length us, event | category | flops | bytes accessed | tf_op | source)
XLA Modules:
  0.0 446.4 jit_solution(11342091478653983375)
XLA Ops:
  0.7 3.9 fusion.67
  4.5 2.6 collective-permute-start.1
  7.1 3.9 collective-permute-start
  11.0 3.0 pad_maximum_fusion.2
  30.2 32.2 %collective-permute-done.5 = bf16[4,8,16,768]{3,2,1,0:T(8,128)(2,1)} collective-permute-done((bf16[4,8,16,768]{3,2,1,0:T(8,128)(2,1)}, bf16[4,8,16,768]{3,2,1,0:T(8,128)(2,1)}, u32[]{:S(2)}, u32[]{:S(2)}) %collective-permute-start.5) | collective-permute-done | bytes 786464 | tf_op jit(solution)/shard_map/ppermute | solution.py:156
  64.5 11.0 %collective-permute-done.6 = bf16[4,8,16,768]{3,2,1,0:T(8,128)(2,1)} collective-permute-done((bf16[4,8,16,768]{3,2,1,0:T(8,128)(2,1)}, bf16[4,8,16,768]{3,2,1,0:T(8,128)(2,1)}, u32[]{:S(2)}, u32[]{:S(2)}) %collective-permute-start.6) | collective-permute-done | bytes 786464 | tf_op jit(solution)/shard_map/ppermute | solution.py:156
  75.5 2.9 collective-permute-start.9
  81.4 33.6 %collective-permute-done.8 = bf16[4,8,16,768]{3,2,1,0:T(8,128)(2,1)S(1)} collective-permute-done((bf16[4,8,16,768]{3,2,1,0:T(8,128)(2,1)S(1)}, bf16[4,8,16,768]{3,2,1,0:T(8,128)(2,1)S(1)}, u32[]{:S(2)}, u32[]{:S(2)}) %collective-permute-start.8) | collective-permute-done | bytes 786464 | tf_op jit(solution)/shard_map/ppermute | solution.py:156
  117.9 6.4 %gather_fusion = bf16[8,4,8,16,768]{4,3,2,1,0:T(8,128)(2,1)} fusion(bf16[8,4,8,16,768]{4,3,2,1,0:T(8,128)(2,1)} %bitcast_dynamic-update-slice_fusion.2, s32[1024]{0:T(1024)S(1)} %pad_clamp_fusion), kind=kCustom, calls=%fused_computation | custom fusion | bytes 12582944 | tf_op jit(solution)/shard_map/gather | solution.py:157
  124.3 6.1 %copy.167 = bf16[4,8,8,16,768]{4,3,2,1,0:T(8,128)(2,1)} copy(bf16[4,8,8,16,768]{4,3,2,0,1:T(8,128)(2,1)} %bitcast.414) | data formatting | bytes 12582912 | tf_op jit(solution)/shard_map/transpose | solution.py:19
  130.4 13.7 %reshape_reshape.4 = bf16[4,64,16,6,128]{4,3,2,1,0:T(8,128)(2,1)} reshape(bf16[4,8,8,16,768]{4,3,2,1,0:T(8,128)(2,1)} %copy.167) | data formatting | bytes 12582912 | tf_op jit(solution)/shard_map/reshape;reshape | solution.py:161
  144.1 5.5 %fusion.86 = (bf16[1,16,6,64,128]{4,2,1,3,0:T(8,128)(2,1)S(1)}, bf16[1,16,6,64,128]{4,2,1,3,0:T(8,128)(2,1)S(1)}, bf16[1,16,6,64,128]{4,2,1,3,0:T(8,128)(2,1)S(1)}, bf16[1,16,6,64,128]{4,2,1,3,0:T(8,128)(2,1)S(1)}) fusion(bf16[4,16,6,64,128]{4,2,1,3,0:T(8,128)(2,1)} %bitcast.412), kind=kLoop, calls=%fused_computation.163 | loop fusion | bytes 12582912 | tf_op jit(solution)/shard_map/slice | solution.py:165
  156.0 3.2 fusion.90
  159.2 3.1 convolution_convert_fusion.1
  171.7 4.6 %maximum_bitcast_fusion = bf16[4,64,16,6,128]{4,3,2,1,0:T(8,128)(2,1)} fusion(bf16[1,16,6,64,128]{4,2,1,3,0:T(8,128)(2,1)S(1)} %copy.178, bf16[1,16,6,64,128]{4,2,1,3,0:T(8,128)(2,1)S(1)} %copy.177, bf16[1,16,6,64,128]{4,2,1,3,0:T(8,128)(2,1)S(1)} %copy.176, bf16[1,16,6,64,128]{4,2,1,3,0:T(8,128)(2,1)S(1)} %copy.175), kind=kLoop, calls=%fused_computation.102 | loop fusion | flops 9437184 | bytes 12582912 | tf_op jit(solution)/shard_map/transpose | solution.py:170
  176.3 13.9 %reshape.602 = bf16[4,64,16,768]{3,2,1,0:T(8,128)(2,1)} reshape(bf16[4,64,16,6,128]{4,3,2,1,0:T(8,128)(2,1)} %maximum_bitcast_fusion) | data formatting | bytes 12582912 | tf_op jit(solution)/shard_map/reshape | solution.py:171
  190.2 6.3 %copy.179 = bf16[4,64,16,768]{3,2,0,1:T(8,128)(2,1)} copy(bf16[4,64,16,768]{3,2,1,0:T(8,128)(2,1)} %reshape.602) | data formatting | bytes 12582912 | tf_op jit(solution)/shard_map/reshape | solution.py:171
  196.5 5.0 %all-to-all-start = ((bf16[4,64,16,768]{3,2,0,1:T(8,128)(2,1)}), bf16[4,64,16,768]{3,2,0,1:T(8,128)(2,1)}, u32[]{:S(2)}, u32[]{:S(2)}) async-start(bf16[4,64,16,768]{3,2,0,1:T(8,128)(2,1)} %copy.179), calls=%async_computation | async-start | bytes 12582912 | tf_op jit(solution)/shard_map/all_to_all | solution.py:172
  201.5 5.0 %pad_maximum_fusion.1 = bf16[2,2048,768]{2,1,0:T(8,128)(2,1)} fusion(bf16[2,512,768]{2,1,0:T(8,128)(2,1)} %collective-permute-done.1, bf16[1,1024,768]{2,1,0:T(8,128)(2,1)S(1)} %bitcast.424, bf16[1,1024,768]{2,1,0:T(8,128)(2,1)S(1)} %bitcast.422, bf16[2,512,768]{2,1,0:T(8,128)(2,1)} %collective-permute-done), kind=kLoop, calls=%fused_computation.103 | loop fusion | flops 25165824 | bytes 12582912 | tf_op jit(solution)/shard_map/concatenate | solution.py:31
  206.5 8.7 %copy.152 = bf16[2,2048,768]{1,2,0:T(8,128)(2,1)} copy(bf16[2,2048,768]{2,1,0:T(8,128)(2,1)} %pad_maximum_fusion.1) | data formatting | bytes 12582912 | tf_op jit(solution)/shard_map/concatenate | solution.py:31
  215.2 7.8 %copy.228 = bf16[192,8,16,128]{3,2,1,0:T(8,128)(2,1)} copy(bf16[192,8,16,128]{3,1,2,0:T(8,128)(2,1)} %bitcast.415) | data formatting | bytes 12582912
  223.1 157.3 %while.29 = (s32[]{:T(128)}, bf16[6,8,128,128]{2,3,1,0:T(8,128)(2,1)}, bf16[6,8,128,128]{3,2,1,0:T(8,128)(2,1)}, f32[6,2,16,128,128]{4,3,2,1,0:T(8,128)}, bf16[6...) while((s32[]{:T(128)}, ...), condition=%wide.region_4.5_spmd.clone, body=%wide.region_0.4_spmd.clone.sunk | while | flops 1831469184 | bytes 212113696 | solution.py:102
  226.5 2.4 fusion.166
  230.3 5.6 %fusion.167 = (f32[8,128]{1,0:T(8,128)S(1)}, f32[8,128,1152]{2,1,0:T(8,128)}) fusion(bf16[8,1152,128]{2,1,0:T(8,128)(2,1)} %bitcast.410, pred[8,1152]{1,0:T(8,128)(4,1)S(1)} %broadcast_bitcast_fusion.2, bf16[1,8,128,128]{3,2,1,0:T(8,128)(2,1)S(1)} %copy.252), kind=kOutput, calls=%fused_computation.162.clone.1 | convolution fusion | flops 307889280 | bytes 7353344 | tf_op jit(solution)/shard_map/while/body/eval_jaxpr/sub | solution.py:48
  235.9 3.0 fusion.168
  252.6 2.4 fusion.166
  256.4 5.6 %fusion.167 = (f32[8,128]{1,0:T(8,128)S(1)}, f32[8,128,1152]{2,1,0:T(8,128)}) fusion(bf16[8,1152,128]{2,1,0:T(8,128)(2,1)} %bitcast.410, pred[8,1152]{1,0:T(8,128)(4,1)S(1)} %broadcast_bitcast_fusion.2, bf16[1,8,128,128]{3,2,1,0:T(8,128)(2,1)S(1)} %copy.252), kind=kOutput, calls=%fused_computation.162.clone.1 | convolution fusion | flops 307889280 | bytes 7353344 | tf_op jit(solution)/shard_map/while/body/eval_jaxpr/sub | solution.py:48
  262.0 3.0 fusion.168
  282.5 5.6 %fusion.167 = (f32[8,128]{1,0:T(8,128)S(1)}, f32[8,128,1152]{2,1,0:T(8,128)}) fusion(bf16[8,1152,128]{2,1,0:T(8,128)(2,1)} %bitcast.410, pred[8,1152]{1,0:T(8,128)(4,1)S(1)} %broadcast_bitcast_fusion.2, bf16[1,8,128,128]{3,2,1,0:T(8,128)(2,1)S(1)} %copy.252), kind=kOutput, calls=%fused_computation.162.clone.1 | convolution fusion | flops 307889280 | bytes 7353344 | tf_op jit(solution)/shard_map/while/body/eval_jaxpr/sub | solution.py:48
  288.1 3.0 fusion.168
  304.9 2.4 fusion.166
  308.6 5.6 %fusion.167 = (f32[8,128]{1,0:T(8,128)S(1)}, f32[8,128,1152]{2,1,0:T(8,128)}) fusion(bf16[8,1152,128]{2,1,0:T(8,128)(2,1)} %bitcast.410, pred[8,1152]{1,0:T(8,128)(4,1)S(1)} %broadcast_bitcast_fusion.2, bf16[1,8,128,128]{3,2,1,0:T(8,128)(2,1)S(1)} %copy.252), kind=kOutput, calls=%fused_computation.162.clone.1 | convolution fusion | flops 307889280 | bytes 7353344 | tf_op jit(solution)/shard_map/while/body/eval_jaxpr/sub | solution.py:48
  314.3 3.0 fusion.168
  331.0 2.4 fusion.166
  334.8 5.6 %fusion.167 = (f32[8,128]{1,0:T(8,128)S(1)}, f32[8,128,1152]{2,1,0:T(8,128)}) fusion(bf16[8,1152,128]{2,1,0:T(8,128)(2,1)} %bitcast.410, pred[8,1152]{1,0:T(8,128)(4,1)S(1)} %broadcast_bitcast_fusion.2, bf16[1,8,128,128]{3,2,1,0:T(8,128)(2,1)S(1)} %copy.252), kind=kOutput, calls=%fused_computation.162.clone.1 | convolution fusion | flops 307889280 | bytes 7353344 | tf_op jit(solution)/shard_map/while/body/eval_jaxpr/sub | solution.py:48
  340.4 3.0 fusion.168
  357.1 2.4 fusion.166
  360.9 5.6 %fusion.167 = (f32[8,128]{1,0:T(8,128)S(1)}, f32[8,128,1152]{2,1,0:T(8,128)}) fusion(bf16[8,1152,128]{2,1,0:T(8,128)(2,1)} %bitcast.410, pred[8,1152]{1,0:T(8,128)(4,1)S(1)} %broadcast_bitcast_fusion.2, bf16[1,8,128,128]{3,2,1,0:T(8,128)(2,1)S(1)} %copy.252), kind=kOutput, calls=%fused_computation.162.clone.1 | convolution fusion | flops 307889280 | bytes 7353344 | tf_op jit(solution)/shard_map/while/body/eval_jaxpr/sub | solution.py:48
  366.5 3.0 fusion.168
  380.3 6.2 %convert.4 = bf16[6,2,16,128,128]{4,3,2,1,0:T(8,128)(2,1)S(1)} convert(f32[6,2,16,128,128]{4,3,2,1,0:T(8,128)} %get-tuple-element.300) | non-fusion elementwise | flops 3145728 | bytes 18874368 | tf_op jit(solution)/shard_map/convert.1
  390.3 4.7 %collective-permute-start.3 = (bf16[6,2,4,128,128]{4,3,2,1,0:T(8,128)(2,1)}, bf16[6,2,4,128,128]{4,3,2,1,0:T(8,128)(2,1)}, u32[]{:S(2)}, u32[]{:S(2)}) collective-permute-start(bf16[6,2,4,128,128]{4,3,2,1,0:T(8,128)(2,1)} %get-tuple-element.415), channel_id=1, source_target_pairs={{0,4},{4,8},{8,12},{12,16},{16,20},{20,24},{24,28},{1,5},{5,9},{9,... | collective-permute-start | bytes 4718600 | tf_op jit(solution)/shard_map/ppermute | solution.py:38
  395.0 6.3 %slice.552 = f32[6,2,8,128,128]{4,3,2,1,0:T(8,128)} slice(f32[6,2,16,128,128]{4,3,2,1,0:T(8,128)} %get-tuple-element.300), slice={[0:6], [0:2], [4:12], [0:128], [0:128]} | slice | bytes 12582912 | tf_op jit(solution)/shard_map/slice | solution.py:135
  402.4 3.9 copy.197
  406.3 4.4 copy_bitcast_fusion.5
  410.7 15.9 %collective-permute-done.2 = bf16[6,2,4,128,128]{4,3,2,1,0:T(8,128)(2,1)} collective-permute-done((bf16[6,2,4,128,128]{4,3,2,1,0:T(8,128)(2,1)}, bf16[6,2,4,128,128]{4,3,2,1,0:T(8,128)(2,1)}, u32[]{:S(2)}, u32[]{:S(2)}) %collective-permute-start.2) | collective-permute-done | bytes 1572896 | tf_op jit(solution)/shard_map/ppermute | solution.py:38
  426.5 2.8 add_dynamic-update-slice_fusion
  434.7 2.6 copy_bitcast_fusion.3
  437.3 3.4 copy.180
  (331 shorter events, 147.5 us)
Async XLA Ops:
  0.6 10.4 %copy-start.5 = (bf16[1024,768]{1,0:T(8,128)(2,1)S(1)}, bf16[1024,768]{1,0:T(8,128)(2,1)}, u32[]{:S(2)}) copy-start(bf16[1024,768]{1,0:T(8,128)(2,1)} %param.42) | copy-start | bytes 4718596
  0.6 10.4 %copy-start.6 = (bf16[1024,768]{1,0:T(8,128)(2,1)S(1)}, bf16[1024,768]{1,0:T(8,128)(2,1)}, u32[]{:S(2)}) copy-start(bf16[1024,768]{1,0:T(8,128)(2,1)} %param.41) | copy-start | bytes 4718596
  4.5 197.0 %collective-permute-start.1 = (bf16[2,512,768]{2,1,0:T(8,128)(2,1)}, bf16[2,512,768]{2,1,0:T(8,128)(2,1)}, u32[]{:S(2)}, u32[]{:S(2)}) collective-permute-start(bf16[2,512,768]{2,1,0:T(8,128)(2,1)} %get-tuple-element.420), channel_id=1, source_target_pairs={{4,0},{8,4},{12,8},{16,12},{20,16},{24,20},{28,24},{5,1},{9,5},{13... | collective-permute-start | bytes 4718600 | tf_op jit(solution)/shard_map/ppermute | solution.py:30
  7.1 194.4 %collective-permute-start = (bf16[2,512,768]{2,1,0:T(8,128)(2,1)}, bf16[2,512,768]{2,1,0:T(8,128)(2,1)}, u32[]{:S(2)}, u32[]{:S(2)}) collective-permute-start(bf16[2,512,768]{2,1,0:T(8,128)(2,1)} %get-tuple-element.419), channel_id=1, source_target_pairs={{0,4},{4,8},{8,12},{12,16},{16,20},{20,24},{24,28},{1,5},{5,9},{9,... | collective-permute-start | bytes 4718600 | tf_op jit(solution)/shard_map/ppermute | solution.py:29
  14.0 4.3 copy-start.2
  14.0 8.6 %copy-start.15 = (s32[64,64]{1,0:T(8,128)S(1)}, s32[64,64]{1,0:T(8,128)}, u32[]{:S(2)}) copy-start(s32[64,64]{1,0:T(8,128)} %param.43) | copy-start | bytes 49156
  14.1 8.7 %copy-start.10 = (bf16[1024,768]{1,0:T(8,128)(2,1)S(1)}, bf16[1024,768]{1,0:T(8,128)(2,1)}, u32[]{:S(2)}) copy-start(bf16[1024,768]{1,0:T(8,128)(2,1)} %param.34) | copy-start | bytes 4718596
  18.4 9.3 %collective-permute-start.4 = (bf16[4,8,16,768]{3,2,1,0:T(8,128)(2,1)}, bf16[4,8,16,768]{3,2,1,0:T(8,128)(2,1)}, u32[]{:S(2)}, u32[]{:S(2)}) collective-permute-start(bf16[4,8,16,768]{3,2,1,0:T(8,128)(2,1)} %get-tuple-element.414), channel_id=1, source_target_pairs={{0,4},{4,0},{8,12},{12,8},{16,20},{20,16},{24,28},{28,24},{1,5},{5... | collective-permute-start | bytes 2359304 | tf_op jit(solution)/shard_map/ppermute | solution.py:156
  18.4 44.0 %collective-permute-start.5 = (bf16[4,8,16,768]{3,2,1,0:T(8,128)(2,1)}, bf16[4,8,16,768]{3,2,1,0:T(8,128)(2,1)}, u32[]{:S(2)}, u32[]{:S(2)}) collective-permute-start(bf16[4,8,16,768]{3,2,1,0:T(8,128)(2,1)} %get-tuple-element.413), channel_id=1, source_target_pairs={{0,8},{4,12},{8,0},{12,4},{16,24},{20,28},{24,16},{28,20},{1,9},{5... | collective-permute-start | bytes 2359304 | tf_op jit(solution)/shard_map/ppermute | solution.py:156
  18.4 57.1 %collective-permute-start.6 = (bf16[4,8,16,768]{3,2,1,0:T(8,128)(2,1)}, bf16[4,8,16,768]{3,2,1,0:T(8,128)(2,1)}, u32[]{:S(2)}, u32[]{:S(2)}) collective-permute-start(bf16[4,8,16,768]{3,2,1,0:T(8,128)(2,1)} %get-tuple-element.412), channel_id=1, source_target_pairs={{0,12},{4,8},{8,4},{12,0},{16,28},{20,24},{24,20},{28,16},{1,13},{... | collective-permute-start | bytes 2359304 | tf_op jit(solution)/shard_map/ppermute | solution.py:156
  23.5 1.6 copy-start.11
  25.1 2.5 copy-start.16
  25.9 36.5 %copy-start.14 = (bf16[4,8,16,768]{3,2,1,0:T(8,128)(2,1)S(1)}, bf16[4,8,16,768]{3,2,1,0:T(8,128)(2,1)}, u32[]{:S(2)}) copy-start(bf16[4,8,16,768]{3,2,1,0:T(8,128)(2,1)} %get-tuple-element.410) | copy-start | bytes 2359300
  25.9 49.6 %copy-start.13 = (bf16[4,8,16,768]{3,2,1,0:T(8,128)(2,1)S(1)}, bf16[4,8,16,768]{3,2,1,0:T(8,128)(2,1)}, u32[]{:S(2)}) copy-start(bf16[4,8,16,768]{3,2,1,0:T(8,128)(2,1)} %get-tuple-element.409) | copy-start | bytes 2359300
  27.5 53.0 %copy-start.12 = (bf16[4,8,16,768]{3,2,1,0:T(8,128)(2,1)S(1)}, bf16[4,8,16,768]{3,2,1,0:T(8,128)(2,1)}, u32[]{:S(2)}) copy-start(bf16[4,8,16,768]{3,2,1,0:T(8,128)(2,1)} %get-tuple-element.408) | copy-start | bytes 2359300
  27.7 52.8 %collective-permute-start.7 = (bf16[4,8,16,768]{3,2,1,0:T(8,128)(2,1)}, bf16[4,8,16,768]{3,2,1,0:T(8,128)(2,1)S(1)}, u32[]{:S(2)}, u32[]{:S(2)}) collective-permute-start(bf16[4,8,16,768]{3,2,1,0:T(8,128)(2,1)} %get-tuple-element.411), channel_id=1, source_target_pairs={{0,16},{4,20},{8,24},{12,28},{16,0},{20,4},{24,8},{28,12},{1,17},{... | collective-permute-start | bytes 2359304 | tf_op jit(solution)/shard_map/ppermute | solution.py:156
  62.4 52.6 %collective-permute-start.8 = (bf16[4,8,16,768]{3,2,1,0:T(8,128)(2,1)S(1)}, bf16[4,8,16,768]{3,2,1,0:T(8,128)(2,1)S(1)}, u32[]{:S(2)}, u32[]{:S(2)}) collective-permute-start(bf16[4,8,16,768]{3,2,1,0:T(8,128)(2,1)S(1)} %copy-done.14), channel_id=1, source_target_pairs={{0,20},{4,16},{8,28},{12,24},{16,4},{20,0},{24,12},{28,8},{1,21},{... | collective-permute-start | bytes 2359304 | tf_op jit(solution)/shard_map/ppermute | solution.py:156
  75.5 40.5 %collective-permute-start.9 = (bf16[4,8,16,768]{3,2,1,0:T(8,128)(2,1)S(1)}, bf16[4,8,16,768]{3,2,1,0:T(8,128)(2,1)S(1)}, u32[]{:S(2)}, u32[]{:S(2)}) collective-permute-start(bf16[4,8,16,768]{3,2,1,0:T(8,128)(2,1)S(1)} %copy-done.13), channel_id=1, source_target_pairs={{0,24},{4,28},{8,16},{12,20},{16,8},{20,12},{24,0},{28,4},{1,25},{... | collective-permute-start | bytes 2359304 | tf_op jit(solution)/shard_map/ppermute | solution.py:156
  80.4 36.5 %collective-permute-start.10 = (bf16[4,8,16,768]{3,2,1,0:T(8,128)(2,1)S(1)}, bf16[4,8,16,768]{3,2,1,0:T(8,128)(2,1)S(1)}, u32[]{:S(2)}, u32[]{:S(2)}) collective-permute-start(bf16[4,8,16,768]{3,2,1,0:T(8,128)(2,1)S(1)} %copy-done.12), channel_id=1, source_target_pairs={{0,28},{4,24},{8,20},{12,16},{16,12},{20,8},{24,4},{28,0},{1,29},{... | collective-permute-start | bytes 2359304 | tf_op jit(solution)/shard_map/ppermute | solution.py:156
  159.1 3.1 copy-start.8
  159.2 3.3 copy-start.9
  159.2 4.3 copy-start.17
  196.5 5.0 %copy-start.3 = (bf16[1024,768]{1,0:T(8,128)(2,1)S(1)}, bf16[1024,768]{1,0:T(8,128)(2,1)}, u32[]{:S(2)}) copy-start(bf16[1024,768]{1,0:T(8,128)(2,1)} %param.35) | copy-start | bytes 4718596
  196.5 5.0 %copy-start.4 = (bf16[1024,768]{1,0:T(8,128)(2,1)S(1)}, bf16[1024,768]{1,0:T(8,128)(2,1)}, u32[]{:S(2)}) copy-start(bf16[1024,768]{1,0:T(8,128)(2,1)} %param.36) | copy-start | bytes 4718596
  196.5 240.8 %all-to-all-start = ((bf16[4,64,16,768]{3,2,0,1:T(8,128)(2,1)}), bf16[4,64,16,768]{3,2,0,1:T(8,128)(2,1)}, u32[]{:S(2)}, u32[]{:S(2)}) async-start(bf16[4,64,16,768]{3,2,0,1:T(8,128)(2,1)} %copy.179), calls=%async_computation | async-start | bytes 12582912 | tf_op jit(solution)/shard_map/all_to_all | solution.py:172
  235.9 4.8 %slice-start = ((s8[4718592]{0:T(1024)(128)(4,1)}), s8[4194304]{0:T(1024)(128)(4,1)S(1)}, s32[]{:S(2)}) async-start(s8[4718592]{0:T(1024)(128)(4,1)} %bitcast.408), calls=%async_computation.1 | async-start | bytes 8388608 | tf_op jit(solution)/shard_map/while
  235.9 4.8 %slice-start.1 = ((s8[4718592]{0:T(1024)(128)(4,1)}), s8[524288]{0:T(1024)(128)(4,1)S(1)}, s32[]{:S(2)}) async-start(s8[4718592]{0:T(1024)(128)(4,1)} %bitcast.408), calls=%async_computation.2 | async-start | bytes 1048576 | tf_op jit(solution)/shard_map/while
  240.7 1.7 copy-start
  262.0 4.8 %slice-start = ((s8[4718592]{0:T(1024)(128)(4,1)}), s8[4194304]{0:T(1024)(128)(4,1)S(1)}, s32[]{:S(2)}) async-start(s8[4718592]{0:T(1024)(128)(4,1)} %bitcast.408), calls=%async_computation.1 | async-start | bytes 8388608 | tf_op jit(solution)/shard_map/while
  262.0 4.8 %slice-start.1 = ((s8[4718592]{0:T(1024)(128)(4,1)}), s8[524288]{0:T(1024)(128)(4,1)S(1)}, s32[]{:S(2)}) async-start(s8[4718592]{0:T(1024)(128)(4,1)} %bitcast.408), calls=%async_computation.2 | async-start | bytes 1048576 | tf_op jit(solution)/shard_map/while
  266.8 1.7 copy-start
  288.1 4.8 %slice-start = ((s8[4718592]{0:T(1024)(128)(4,1)}), s8[4194304]{0:T(1024)(128)(4,1)S(1)}, s32[]{:S(2)}) async-start(s8[4718592]{0:T(1024)(128)(4,1)} %bitcast.408), calls=%async_computation.1 | async-start | bytes 8388608 | tf_op jit(solution)/shard_map/while
  288.1 4.8 %slice-start.1 = ((s8[4718592]{0:T(1024)(128)(4,1)}), s8[524288]{0:T(1024)(128)(4,1)S(1)}, s32[]{:S(2)}) async-start(s8[4718592]{0:T(1024)(128)(4,1)} %bitcast.408), calls=%async_computation.2 | async-start | bytes 1048576 | tf_op jit(solution)/shard_map/while
  292.9 1.7 copy-start
  314.2 4.8 %slice-start = ((s8[4718592]{0:T(1024)(128)(4,1)}), s8[4194304]{0:T(1024)(128)(4,1)S(1)}, s32[]{:S(2)}) async-start(s8[4718592]{0:T(1024)(128)(4,1)} %bitcast.408), calls=%async_computation.1 | async-start | bytes 8388608 | tf_op jit(solution)/shard_map/while
  314.3 4.8 %slice-start.1 = ((s8[4718592]{0:T(1024)(128)(4,1)}), s8[524288]{0:T(1024)(128)(4,1)S(1)}, s32[]{:S(2)}) async-start(s8[4718592]{0:T(1024)(128)(4,1)} %bitcast.408), calls=%async_computation.2 | async-start | bytes 1048576 | tf_op jit(solution)/shard_map/while
  319.1 1.7 copy-start
  340.4 4.8 %slice-start = ((s8[4718592]{0:T(1024)(128)(4,1)}), s8[4194304]{0:T(1024)(128)(4,1)S(1)}, s32[]{:S(2)}) async-start(s8[4718592]{0:T(1024)(128)(4,1)} %bitcast.408), calls=%async_computation.1 | async-start | bytes 8388608 | tf_op jit(solution)/shard_map/while
  340.4 4.8 %slice-start.1 = ((s8[4718592]{0:T(1024)(128)(4,1)}), s8[524288]{0:T(1024)(128)(4,1)S(1)}, s32[]{:S(2)}) async-start(s8[4718592]{0:T(1024)(128)(4,1)} %bitcast.408), calls=%async_computation.2 | async-start | bytes 1048576 | tf_op jit(solution)/shard_map/while
  345.2 1.7 copy-start
  366.5 4.8 %slice-start = ((s8[4718592]{0:T(1024)(128)(4,1)}), s8[4194304]{0:T(1024)(128)(4,1)S(1)}, s32[]{:S(2)}) async-start(s8[4718592]{0:T(1024)(128)(4,1)} %bitcast.408), calls=%async_computation.1 | async-start | bytes 8388608 | tf_op jit(solution)/shard_map/while
  366.5 4.8 %slice-start.1 = ((s8[4718592]{0:T(1024)(128)(4,1)}), s8[524288]{0:T(1024)(128)(4,1)S(1)}, s32[]{:S(2)}) async-start(s8[4718592]{0:T(1024)(128)(4,1)} %bitcast.408), calls=%async_computation.2 | async-start | bytes 1048576 | tf_op jit(solution)/shard_map/while
  371.3 1.7 copy-start
  388.4 38.1 %collective-permute-start.2 = (bf16[6,2,4,128,128]{4,3,2,1,0:T(8,128)(2,1)}, bf16[6,2,4,128,128]{4,3,2,1,0:T(8,128)(2,1)}, u32[]{:S(2)}, u32[]{:S(2)}) collective-permute-start(bf16[6,2,4,128,128]{4,3,2,1,0:T(8,128)(2,1)} %get-tuple-element.416), channel_id=1, source_target_pairs={{4,0},{8,4},{12,8},{16,12},{20,16},{24,20},{28,24},{5,1},{9,5},{13... | collective-permute-start | bytes 4718600 | tf_op jit(solution)/shard_map/ppermute | solution.py:38
  390.3 11.0 %copy-start.7 = (bf16[6,8,128,128]{3,2,1,0:T(8,128)(2,1)S(1)}, bf16[6,8,128,128]{3,2,1,0:T(8,128)(2,1)}, u32[]{:S(2)}) copy-start(bf16[6,8,128,128]{3,2,1,0:T(8,128)(2,1)} %get-tuple-element.299) | copy-start | bytes 4718596
  390.3 39.0 %collective-permute-start.3 = (bf16[6,2,4,128,128]{4,3,2,1,0:T(8,128)(2,1)}, bf16[6,2,4,128,128]{4,3,2,1,0:T(8,128)(2,1)}, u32[]{:S(2)}, u32[]{:S(2)}) collective-permute-start(bf16[6,2,4,128,128]{4,3,2,1,0:T(8,128)(2,1)} %get-tuple-element.415), channel_id=1, source_target_pairs={{0,4},{4,8},{8,12},{12,16},{16,20},{20,24},{24,28},{1,5},{5,9},{9,... | collective-permute-start | bytes 4718600 | tf_op jit(solution)/shard_map/ppermute | solution.py:38
  406.3 20.2 %copy-start.1 = (f32[6,2,8,128,128]{4,3,2,1,0:T(8,128)S(1)}, f32[6,2,8,128,128]{4,3,2,1,0:T(8,128)}, u32[]{:S(2)}) copy-start(f32[6,2,8,128,128]{4,3,2,1,0:T(8,128)} %slice.552) | copy-start | bytes 18874372
